TPU v7x, 256 devices: a whole 4x4x8 slice. The times are simulated.
256 devices in a mesh: dp: 2 (over core), ctx: 16 (over z, x_hi), tp: 8 (over y, x_lo).
Axes of the slice: x: 4 (x_hi: 2, x_lo: 2; x = x_hi * 2 + x_lo), y: 4, z: 8, core: 2. Of those that a mesh axis runs over, the one named last changes fastest.
Arguments:
- queries: bfloat16 [2, 4096, 2048], P('dp', 'ctx', 'tp'), may hold values from -32 to 32
- key_heads: bfloat16 [2, 4096, 2048], P('dp', 'ctx', 'tp'), may hold values from -32 to 32
- value_heads: bfloat16 [2, 4096, 2048], P('dp', 'ctx', 'tp'), may hold values from -6 to 6
- grad_output: bfloat16 [2, 4096, 4096], P('dp', 'ctx', 'tp'), may hold values from -6 to 6
- out_weight: bfloat16 [2048, 4096], P('tp'), may hold values from -0.375 to 0.375
- block_pattern: int32 [16, 3], replicated, may hold values from 0 to 15, all different within a row; in each aligned block of 16 rows (0 to 15, 16 to 31, ...) at most 6 rows name the same one
- global_offsets: int32 [16, 8], replicated, may hold values from 0 to 255, as said below
Outputs:
- grad_queries: bfloat16 [2, 4096, 2048], P('dp', 'ctx', 'tp')
- grad_keys: bfloat16 [2, 4096, 2048], P('dp', 'ctx', 'tp')
- grad_values: bfloat16 [2, 4096, 2048], P('dp', 'ctx', 'tp')
- grad_weight: bfloat16 [2048, 4096], P('tp', ('dp', 'ctx'))
Inputs may be any that keep to these rules, and one draw needn't show every extreme that they name: `block_pattern`: each row names 3 different blocks; no block is named by more than 6 rows in all, and one block is named by exactly 6 rows. A row may name its own block or a neighbour. `global_offsets`: row b holds the positions within block b of its 8 global tokens, all different.
All inputs are finite; a program needn't handle non-finite values.
Results may differ from a plain program's by a relative error of at most 0.017.
Values may be sent and summed in bfloat16 or wider, within the bound.
A program may use at most 64 MiB of HBM per device.

v0:
```python
import functools

import jax
import jax.numpy as jnp
from jax import lax
from jax.experimental import pallas as pl
from jax.experimental.pallas import tpu as pltpu
from jax.sharding import PartitionSpec as P

HD = 128
LOWEST = -1e30
SCALE = HD ** (-0.5)
LOG2E = 1.4426950408889634
MESH = pl.DeviceIdType.MESH
F32 = jnp.float32
BF16 = jnp.bfloat16


def nt(a, b):
    return lax.dot_general(a, b, (((1,), (1,)), ((), ())), preferred_element_type=F32)


def tn(a, b):
    return lax.dot_general(a, b, (((0,), (0,)), ((), ())), preferred_element_type=F32)


def nn(a, b):
    return jnp.dot(a, b, preferred_element_type=F32)


def any_of(flags):
    return functools.reduce(jnp.logical_or, flags)


class Sems:
    def __init__(self):
        self.index = {}

    def __getitem__(self, name):
        return self.index.setdefault(name, len(self.index))


N_SEM = 80


def kernel(
    nz,
    ny,
    pat,
    offs,
    q_hbm,
    k_hbm,
    v_hbm,
    g_hbm,
    w_hbm,
    dq_hbm,
    dk_hbm,
    dv_hbm,
    gw_hbm,
    kv,
    q2,
    do2,
    gb,
    wv,
    gh,
    ghb,
    kb,
    qb,
    sb,
    mx,
    lr,
    stat,
    ot,
    ob,
    att,
    pb,
    db,
    own,
    snd,
    rp,
    rm,
    dqt,
    dqb,
    fin,
    gws,
    gwr,
    gwo,
    gsn,
    gp,
    gm,
    gfin,
    gxr,
    gout,
    ss,
    rs,
    ls,
):
    T = q_hbm.shape[1]
    Q2 = 2 * T
    nctx, ntp = 2 * nz, 2 * ny
    DC = g_hbm.shape[2]
    F = w_hbm.shape[0]
    CW = gw_hbm.shape[1]
    GB = offs.shape[1]
    up, dn = nz // 2, max(nz // 2 - 1, 0)
    yup, ydn = ny // 2, max(ny // 2 - 1, 0)
    lanes = [slice(i * 128, (i + 1) * 128) for i in range(Q2 // 128)]

    d = lax.axis_index("dp")
    c = lax.axis_index("ctx")
    t = lax.axis_index("tp")
    z, h = lax.div(c, 2), lax.rem(c, 2)
    y, xl = lax.div(t, 2), lax.rem(t, 2)
    o = 1 - h

    def at_z(step):
        return lax.rem(z + (step + nz), nz)

    def at_y(step):
        return lax.rem(y + (step + ny), ny)

    def zdev(step):
        return (d, at_z(step) * 2 + h, t)

    def ydev(step):
        return (d, c, at_y(step) * 2 + xl)

    partner = (d, 2 * z + o, t)
    xdev = (d, c, 2 * y + 1 - xl)
    core = (1 - d, c, t)
    hcols = pl.ds(pl.multiple_of(h * HD, HD), HD)
    ocols = pl.ds(pl.multiple_of(o * HD, HD), HD)
    hrows = pl.ds(pl.multiple_of(h * T, T), T)
    orows = pl.ds(pl.multiple_of(o * T, T), T)

    sem = Sems()
    sent = []

    def send(name, src, dst, dev):
        i = sem[name]
        cp = pltpu.make_async_remote_copy(
            src_ref=src, dst_ref=dst, send_sem=ss.at[i], recv_sem=rs.at[i],
            device_id=dev, device_id_type=MESH,
        )
        cp.start()
        sent.append(cp)

    def arrive(name, dst):
        i = sem[name]
        pltpu.make_async_remote_copy(
            src_ref=dst, dst_ref=dst, send_sem=ss.at[i], recv_sem=rs.at[i],
            device_id=partner, device_id_type=MESH,
        ).wait_recv()

    def local(i, src, dst):
        cp = pltpu.make_async_copy(src, dst, ls.at[i])
        cp.start()
        return cp

    load_k = local(0, k_hbm.at[0, :, hcols], kv.at[c, 0])
    load_v = local(1, v_hbm.at[0, :, hcols], kv.at[c, 1])
    load_q = local(2, q_hbm.at[0, :, hcols], q2.at[hrows])
    load_g = local(3, g_hbm.at[0], gb.at[t])
    load_w = local(4, w_hbm, wv)

    near = [partner, xdev, core]
    if nz > 1:
        near += [zdev(1), zdev(-1)]
    if ny > 1:
        near += [ydev(1), ydev(-1)]
    barrier = pltpu.get_barrier_semaphore()
    for dev in near:
        pl.semaphore_signal(barrier, inc=1, device_id=dev, device_id_type=MESH)
    pl.semaphore_wait(barrier, len(near))

    hops = {("a", 1): up, ("a", -1): dn, ("b", 1): dn, ("b", -1): up}

    def z_block(chain, step):
        return 2 * at_z(step) + (h if chain == "a" else o)

    def z_send(chain, way, hop):
        if hop < hops[chain, way]:
            block = kv.at[z_block(chain, -way * hop)]
            send(("kv", chain, way, hop + 1), block, block, zdev(way))

    ghops = {("a", 1): yup, ("a", -1): ydn, ("b", 1): ydn, ("b", -1): yup}

    def y_piece(chain, step):
        return 2 * at_y(step) + (xl if chain == "a" else 1 - xl)

    def y_send(chain, way, hop):
        if hop < ghops[chain, way]:
            piece = gb.at[y_piece(chain, -way * hop)]
            src = g_hbm.at[0] if chain == "a" and hop == 0 else piece
            send(("g", chain, way, hop + 1), src, piece, ydev(way))

    send("gx", g_hbm.at[0], gb.at[t], xdev)
    y_send("a", 1, 0)
    y_send("a", -1, 0)
    load_k.wait()
    load_v.wait()
    z_send("a", 1, 0)
    z_send("a", -1, 0)
    send("k", k_hbm.at[0, :, ocols], kv.at[c, 0], partner)
    send("v", v_hbm.at[0, :, ocols], kv.at[c, 1], partner)
    send("q", q_hbm.at[0, :, ocols], q2.at[hrows], partner)

    lane = lax.broadcasted_iota(jnp.int32, (1, Q2), 1)
    is_first = lane < T
    pos = jnp.where(is_first, lane, lane - T)
    b0 = 2 * z
    bvec = jnp.where(is_first, b0, b0 + 1)

    def both(ref, k):
        return jnp.where(is_first, ref[b0, k], ref[b0 + 1, k])

    row_global = any_of([pos == both(offs, g) for g in range(GB)])
    picks = [both(pat, r) for r in range(pat.shape[1])]
    for cc in range(nctx):
        seen = any_of([row_global, jnp.abs(bvec - cc) <= 1] + [pick == cc for pick in picks])
        qb[cc] = jnp.where(seen, 0.0, LOWEST)

    def key_bias(cc, carry):
        row = lax.broadcasted_iota(jnp.int32, (T, 128), 0)
        kb[cc] = jnp.where(any_of([row == offs[cc, g] for g in range(GB)]), 0.0, LOWEST)
        return carry

    lax.fori_loop(0, nctx, key_bias, 0)
    mx[...] = jnp.full_like(mx, LOWEST)
    gh[...] = jnp.zeros_like(gh)

    def score(cc):
        s = nt(kv[cc, 0], q2[...])
        bias = kb[cc]
        row_bias = qb[cc]
        for sl in lanes:
            part = s[:, sl] + jnp.maximum(bias, row_bias[:, sl])
            sb[cc, :, sl] = part
            mx[:, sl] = jnp.maximum(mx[:, sl], jnp.max(part.reshape(T // 8, 8, 128), axis=0))

    def project(tt):
        cols = pl.ds(pl.multiple_of(tt * DC, DC), DC)
        gh[...] += nt(gb[tt], wv[:, cols])

    ready = {"q": False, "blocks": []}

    def scores_of(cc):
        if ready["q"]:
            score(cc)
        else:
            ready["blocks"].append(cc)

    def on_own():
        load_g.wait()
        load_w.wait()
        project(t)
        scores_of(z_block("a", 0))

    def on_q():
        load_q.wait()
        arrive("q", q2.at[orows])
        ready["q"] = True
        for cc in ready["blocks"]:
            score(cc)

    def on_pair():
        pair = z_block("b", 0)
        arrive("k", kv.at[pair, 0])
        arrive("v", kv.at[pair, 1])
        z_send("b", 1, 0)
        z_send("b", -1, 0)
        scores_of(pair)

    def on_gx():
        piece = y_piece("b", 0)
        arrive("gx", gb.at[piece])
        y_send("b", 1, 0)
        y_send("b", -1, 0)
        project(piece)

    def on_kv(chain, way, hop):
        block = z_block(chain, -way * hop)
        arrive(("kv", chain, way, hop), kv.at[block])
        z_send(chain, way, hop)
        scores_of(block)

    def on_g(chain, way, hop):
        piece = y_piece(chain, -way * hop)
        arrive(("g", chain, way, hop), gb.at[piece])
        y_send(chain, way, hop)
        project(piece)

    events = [(0.0, on_own), (7.0, on_gx), (12.5, on_pair), (15.0, on_q)]
    for (chain, way), count in hops.items():
        for hop in range(1, count + 1):
            when = (0.0 if chain == "a" else 12.6) + 4.5 * hop
            events.append((when, functools.partial(on_kv, chain, way, hop)))
    for (chain, way), count in ghops.items():
        for hop in range(1, count + 1):
            when = (0.0 if chain == "a" else 7.1) + 7.2 * hop
            events.append((when, functools.partial(on_g, chain, way, hop)))
    for _, event in sorted(events, key=lambda pair: pair[0]):
        event()

    ghb[0] = gh[:, :HD].astype(BF16)
    ghb[1] = gh[:, HD:].astype(BF16)
    send("do", ghb.at[o], do2.at[hrows], partner)
    do2[hrows, :] = ghb[h]

    stat[0] = jnp.max(mx[...], axis=0, keepdims=True)
    lr[...] = jnp.zeros_like(lr)
    ot[...] = jnp.zeros_like(ot)

    def weigh(cc, carry):
        for sl in lanes:
            e = jnp.exp2((sb[cc, :, sl] - stat[0, :, sl]) * (SCALE * LOG2E))
            sb[cc, :, sl] = e
            lr[:, sl] += jnp.sum(e.reshape(T // 8, 8, 128), axis=0)
            pb[:, sl] = e.astype(BF16)
        ot[...] += tn(kv[cc, 1], pb[...])
        return carry

    lax.fori_loop(0, nctx, weigh, 0)
    inverse = 1.0 / jnp.sum(lr[...], axis=0, keepdims=True)
    stat[1] = inverse
    low = (ot[...] * inverse).astype(BF16)
    ob[...] = low
    send("att", ob.at[:, orows], att.at[h], partner)
    att[h] = ob[:, hrows]
    arrive("do", do2.at[orows])
    do_t = jnp.transpose(do2[...].astype(F32))
    stat[2] = jnp.sum(do_t * low.astype(F32), axis=0, keepdims=True)
    dqt[...] = jnp.zeros_like(dqt)

    def gradients(zz):
        def one(x, carry):
            cc = 2 * zz + x
            dp = nt(kv[cc, 1], do2[...])
            for sl in lanes:
                p = sb[cc, :, sl] * stat[1, :, sl]
                pb[:, sl] = p.astype(BF16)
                db[:, sl] = (p * (dp[:, sl] - stat[2, :, sl])).astype(BF16)
            own[zz, 0, x] = SCALE * nn(db[...], q2[...])
            own[zz, 1, x] = nn(pb[...], do2[...])
            dqt[...] += tn(kv[cc, 0], db[...])
            return carry

        lax.fori_loop(0, 2, one, 0)

    first_hop = {(0, 1): up, (0, -1): dn, (1, 1): dn, (1, -1): up}
    slots = {1: rp, -1: rm}

    def pass_on(i, way, hop):
        zz = at_z(way * hop)
        total = own[zz, i]
        if hop < first_hop[i, way]:
            slot = slots[way].at[i, hop]
            arrive(("kvg", i, way, hop + 1), slot)
            total = total + slot[...].astype(F32)
        snd[zz, i] = total.astype(BF16)
        send(("kvg", i, way, hop), snd.at[zz, i], slots[way].at[i, hop - 1], zdev(way))

    half = ntp // 2
    per_piece = DC // CW

    def weight_part(part, base, out):
        piece = base * half + part
        for head in range(2):
            rows = slice(head * HD, (head + 1) * HD)
            res = nn(att[head], gb[piece])
            for j in range(per_piece):
                out[part * per_piece + j, rows] = res[:, j * CW:(j + 1) * CW].astype(out.dtype)

    def weight_other():
        arrive("att", att.at[o])

        def one(part, carry):
            weight_part(part, 1 - d, gws)
            return carry

        lax.fori_loop(0, half, one, 0)
        send("gw", gws, gwr, core)

    def weight_own():
        def one(part, carry):
            weight_part(part, d, gwo)
            return carry

        lax.fori_loop(0, half, one, 0)

    gslots = {1: gp, -1: gm}

    def weight_sum(zz, x):
        return gwo[2 * zz + x] + gwr[2 * zz + x].astype(F32)

    def weight_far():
        zz = at_z(up)
        for x, way in ((0, 1), (1, -1)):
            gsn[zz, x] = weight_sum(zz, x).astype(BF16)
            send(("gwz", way, up), gsn.at[zz, x], gslots[way].at[up - 1, x], zdev(way))

    def weight_arrive(way, hop):
        if hop == up:
            x = 0 if way == 1 else 1
            arrive(("gwz", way, hop), gslots[way].at[hop - 1, x])
            return [x]
        arrive(("gwz", way, hop), gslots[way].at[hop - 1])
        return [0, 1]

    def weight_pass(way, hop):
        zz = at_z(way * hop)
        halves = weight_arrive(way, hop + 1)
        for x in range(2):
            total = weight_sum(zz, x)
            if x in halves:
                total = total + gslots[way][hop, x].astype(F32)
            gsn[zz, x] = total.astype(BF16)
        send(("gwz", way, hop), gsn.at[zz], gslots[way].at[hop - 1], zdev(way))

    if nz > 1:
        gradients(at_z(up))
        pass_on(0, 1, up)
        pass_on(1, -1, up)
    if dn:
        gradients(at_z(dn))
        gradients(at_z(-dn))
    weight_other()
    late = []
    for hop in range(dn, 0, -1):
        if hop < dn:
            gradients(at_z(hop))
            gradients(at_z(-hop))
        for i in ((1, 0) if hop == dn else (0, 1)):
            pass_on(i, 1, hop)
            pass_on(1 - i, -1, hop)
        if hop == dn:
            weight_own()
        elif hop == dn - 1:
            arrive("gw", gwr)
            weight_far()
        else:
            weight_pass(1, hop + 2)
            weight_pass(-1, hop + 2)
    gradients(z)
    if dn == 0:
        weight_own()
    if dn < 2:
        arrive("gw", gwr)
        if nz > 1:
            weight_far()
        rest = range(dn, 0, -1)
    else:
        rest = range(2, 0, -1)

    dqb[...] = jnp.transpose(SCALE * dqt[...]).astype(BF16)
    send("dq", dqb.at[orows], dq_hbm.at[0, :, hcols], partner)
    out_q = local(2, dqb.at[hrows], dq_hbm.at[0, :, hcols])

    if len(rest) and dn:
        weight_pass(1, rest[0])
        weight_pass(-1, rest[0])

    outs = [out_q]
    for i, out in ((0, dk_hbm), (1, dv_hbm)):
        total = own[z, i]
        for way in (1, -1):
            if first_hop[i, way] > 0:
                arrive(("kvg", i, way, 1), slots[way].at[i, 0])
                total = total + slots[way][i, 0].astype(F32)
        fin[i] = total.astype(BF16)
        send(("fin", i), fin.at[i, o], out.at[0, :, hcols], partner)
        outs.append(local(i, fin.at[i, h], out.at[0, :, hcols]))

    for hop in rest[1:]:
        weight_pass(1, hop)
        weight_pass(-1, hop)
    tops = [weight_sum(z, 0), weight_sum(z, 1)]
    if nz > 1:
        for way in (1, -1):
            for x in weight_arrive(way, 1):
                tops[x] = tops[x] + gslots[way][0, x].astype(F32)
    gfin[0] = tops[0]
    gfin[1] = tops[1]
    gsn[z, 0] = gfin[o].astype(BF16)
    send("gwx", gsn.at[z, 0], gxr, partner)
    arrive("gwx", gxr)
    gout[...] = (gfin[h] + gxr[...].astype(F32)).astype(BF16)
    outs.append(local(3, gout, gw_hbm))

    arrive("dq", dq_hbm.at[0, :, ocols])
    arrive(("fin", 0), dk_hbm.at[0, :, ocols])
    arrive(("fin", 1), dv_hbm.at[0, :, ocols])
    for cp in outs:
        cp.wait()
    for cp in sent:
        cp.wait_send()
    assert len(sem.index) <= N_SEM


def per_device(nz, ny, q, k, v, g, w, pattern, offsets):
    T = q.shape[1]
    Q2 = 2 * T
    nctx, ntp = 2 * nz, 2 * ny
    DC, F = g.shape[2], w.shape[0]
    CW = w.shape[1] // (2 * nctx)
    deep = max(nz // 2, 1)
    V = pltpu.VMEM
    hbm = pl.BlockSpec(memory_space=pl.ANY)
    smem = pl.BlockSpec(memory_space=pltpu.SMEM)
    scratch = [
        V((nctx, 2, T, HD), BF16),
        V((Q2, HD), BF16),
        V((Q2, HD), BF16),
        V((ntp, T, DC), BF16),
        V(w.shape, BF16),
        V((T, F), F32),
        V((2, T, HD), BF16),
        V((nctx, T, 128), F32),
        V((nctx, 1, Q2), F32),
        V((nctx, T, Q2), F32),
        V((8, Q2), F32),
        V((8, Q2), F32),
        V((3, 1, Q2), F32),
        V((HD, Q2), F32),
        V((HD, Q2), BF16),
        V((2, HD, T), BF16),
        V((T, Q2), BF16),
        V((T, Q2), BF16),
        V((nz, 2, 2, T, HD), F32),
        V((nz, 2, 2, T, HD), BF16),
        V((2, deep, 2, T, HD), BF16),
        V((2, deep, 2, T, HD), BF16),
        V((HD, Q2), F32),
        V((Q2, HD), BF16),
        V((2, 2, T, HD), BF16),
        V((nctx, F, CW), BF16),
        V((nctx, F, CW), BF16),
        V((nctx, F, CW), F32),
        V((nz, 2, F, CW), BF16),
        V((deep, 2, F, CW), BF16),
        V((deep, 2, F, CW), BF16),
        V((2, F, CW), F32),
        V((F, CW), BF16),
        V((F, CW), BF16),
        pltpu.SemaphoreType.DMA((N_SEM,)),
        pltpu.SemaphoreType.DMA((N_SEM,)),
        pltpu.SemaphoreType.DMA((5,)),
    ]
    like = jax.ShapeDtypeStruct(q.shape, BF16)
    return pl.pallas_call(
        functools.partial(kernel, nz, ny),
        out_shape=(like, like, like, jax.ShapeDtypeStruct((F, CW), BF16)),
        in_specs=[smem, smem, hbm, hbm, hbm, hbm, hbm],
        out_specs=(hbm, hbm, hbm, hbm),
        scratch_shapes=scratch,
        compiler_params=pltpu.CompilerParams(
            collective_id=0, has_side_effects=True, vmem_limit_bytes=60 * 1024 * 1024
        ),
        name="attention_backward",
    )(pattern, offsets, q, k, v, g, w)


def solution(mesh):
    nz, ny = mesh.shape["ctx"] // 2, mesh.shape["tp"] // 2
    spec = P("dp", "ctx", "tp")
    return jax.shard_map(
        functools.partial(per_device, nz, ny),
        mesh=mesh,
        in_specs=(spec, spec, spec, spec, P("tp", None), P(), P()),
        out_specs=(spec, spec, spec, P("tp", ("dp", "ctx"))),
        check_vma=False,
    )
```

profile of v0, /device:TPU:2, one launch (start us, length us, event | category | flops | bytes accessed | tf_op | source)
XLA Modules:
  0.0 102.1 jit_solution(11243386637077973592)
XLA Ops:
  0.6 1.4 %copy.11.pat = s32[16,3]{1,0:T(8,128)} copy(s32[16,3]{0,1:T(4,128)} %param.12) | data formatting | bytes 384 | tf_op args[5]
  2.0 1.4 %copy.12.offs = s32[16,8]{1,0:T(8,128)} copy(s32[16,8]{0,1:T(8,128)} %param.13) | data formatting | bytes 1024 | tf_op args[6]
  3.3 92.6 %attention_backward.1 = (bf16[1,256,256]{2,1,0:T(8,128)(2,1)}, bf16[1,256,256]{2,1,0:T(8,128)(2,1)}, bf16[1,256,256]{2,1,0:T(8,128)(2,1)}, bf16[256,128]{1,0:T(8,128)(2,1)}) custom-call(s32[16,3]{1,0:T(8,128)} %copy.11.pat, s32[16,8]{1,0:T(8,128)} %copy.12.offs, bf16[1,256,256]{2,1,0:T(8,128)(2,1)} %q_hbm.1, bf16[1,256,256]{2,1,0:T(8,128)(2,1)} %k_hbm.1, ...), custom_call_target="tpu_custom_call" | custom-call | tf_op jit(solution)/shard_map/attention_backward/pallas_call | solution.py:550
  95.9 1.6 %copy.17 = bf16[1,256,256]{2,1,0:T(8,128)(2,1)} copy(bf16[1,256,256]{2,1,0:T(8,128)(2,1)} %get-tuple-element.8) | data formatting | bytes 262144
  97.5 1.6 %copy.18 = bf16[1,256,256]{2,1,0:T(8,128)(2,1)} copy(bf16[1,256,256]{2,1,0:T(8,128)(2,1)} %get-tuple-element.9) | data formatting | bytes 262144
  99.1 1.6 %copy.19 = bf16[1,256,256]{2,1,0:T(8,128)(2,1)} copy(bf16[1,256,256]{2,1,0:T(8,128)(2,1)} %get-tuple-element.10) | data formatting | bytes 262144
  100.6 1.5 %copy.20 = bf16[256,128]{1,0:T(8,128)(2,1)} copy(bf16[256,128]{1,0:T(8,128)(2,1)} %get-tuple-element.11) | data formatting | bytes 131072
where the time goes:
time: 102 us
  Pallas kernels  92.6 us (91%)
  local copies, waits for them, and re-layouts  8.88 us (9%)
    pallas_call x1, Pallas kernels, per_device(): pl.pallas_call(functools.partial(kernel, nz, ny), out_shape=(like, like,...  92.6 us
    unnamed x6, local copies, waits for them, and re-layouts  8.88 us

commit v1 on v0

v1 whole, which is shorter than its diff:
```python
import functools

import jax
import jax.numpy as jnp
from jax import lax
from jax.experimental import pallas as pl
from jax.experimental.pallas import tpu as pltpu
from jax.sharding import PartitionSpec as P

HD = 128
LOWEST = -1e30
SCALE = HD ** (-0.5)
LOG2E = 1.4426950408889634
MESH = pl.DeviceIdType.MESH
F32 = jnp.float32
BF16 = jnp.bfloat16


def nt(a, b):
    return lax.dot_general(a, b, (((1,), (1,)), ((), ())), preferred_element_type=F32)


def tn(a, b):
    return lax.dot_general(a, b, (((0,), (0,)), ((), ())), preferred_element_type=F32)


def nn(a, b):
    return jnp.dot(a, b, preferred_element_type=F32)


def any_of(flags):
    return functools.reduce(jnp.logical_or, flags)


class Sems:
    def __init__(self):
        self.index = {}

    def __getitem__(self, name):
        return self.index.setdefault(name, len(self.index))


N_SEM = 110


def arrival_times(flows):
    done, free = {}, {}
    left = dict(flows)
    while left:
        ready = []
        for name, (needs, delay, link, busy, wait) in left.items():
            if all(n in done for n in needs):
                start = max([done[n] for n in needs] + [0.0]) + delay
                ready.append((start, len(ready), name))
        start, _, name = min(ready)
        _, _, link, busy, wait = left.pop(name)
        begin = max(start, free.get(link, 0.0))
        free[link] = begin + busy
        done[name] = begin + busy + wait
    return done


def kernel(
    nz,
    ny,
    pat,
    offs,
    q_hbm,
    k_hbm,
    v_hbm,
    g_hbm,
    w_hbm,
    dq_hbm,
    dk_hbm,
    dv_hbm,
    gw_hbm,
    kv,
    q2,
    do2,
    gb,
    wv,
    gh,
    ghb,
    kb,
    qb,
    sb,
    mx,
    lr,
    stat,
    ot,
    ob,
    att,
    pb,
    db,
    own,
    snd,
    rp,
    rm,
    dqt,
    dqb,
    fin,
    gws,
    gwr,
    gwo,
    gxs,
    gxr,
    gsn,
    gp,
    gm,
    gout,
    ss,
    rs,
    ls,
):
    T = q_hbm.shape[1]
    Q2 = 2 * T
    nctx, ntp = 2 * nz, 2 * ny
    DC = g_hbm.shape[2]
    F = w_hbm.shape[0]
    CW = gw_hbm.shape[1]
    GB = offs.shape[0]
    up, dn = nz // 2, max(nz // 2 - 1, 0)
    yup, ydn = ny // 2, max(ny // 2 - 1, 0)
    lanes = [slice(i * 128, (i + 1) * 128) for i in range(Q2 // 128)]

    d = lax.axis_index("dp")
    c = lax.axis_index("ctx")
    t = lax.axis_index("tp")
    z, h = lax.div(c, 2), lax.rem(c, 2)
    y, xl = lax.div(t, 2), lax.rem(t, 2)
    o = 1 - h

    def at_z(step):
        return lax.rem(z + (step + nz), nz)

    def at_y(step):
        return lax.rem(y + (step + ny), ny)

    def zdev(step):
        return (d, at_z(step) * 2 + h, t)

    def ydev(step):
        return (d, c, at_y(step) * 2 + xl)

    partner = (d, 2 * z + o, t)
    xdev = (d, c, 2 * y + 1 - xl)
    core = (1 - d, c, t)
    hcols = pl.ds(pl.multiple_of(h * HD, HD), HD)
    ocols = pl.ds(pl.multiple_of(o * HD, HD), HD)
    hrows = pl.ds(pl.multiple_of(h * T, T), T)
    orows = pl.ds(pl.multiple_of(o * T, T), T)

    sem = Sems()
    sent = []

    def send(name, src, dst, dev):
        i = sem[name]
        cp = pltpu.make_async_remote_copy(
            src_ref=src, dst_ref=dst, send_sem=ss.at[i], recv_sem=rs.at[i],
            device_id=dev, device_id_type=MESH,
        )
        cp.start()
        sent.append(cp)

    def arrive(name, dst):
        i = sem[name]
        pltpu.make_async_remote_copy(
            src_ref=dst, dst_ref=dst, send_sem=ss.at[i], recv_sem=rs.at[i],
            device_id=partner, device_id_type=MESH,
        ).wait_recv()

    def local(i, src, dst):
        cp = pltpu.make_async_copy(src, dst, ls.at[i])
        cp.start()
        return cp

    load_k = local(0, k_hbm.at[0, :, hcols], kv.at[c, 0])
    load_v = local(1, v_hbm.at[0, :, hcols], kv.at[c, 1])
    load_q = local(2, q_hbm.at[0, :, hcols], q2.at[hrows])
    load_g = local(3, g_hbm.at[0], gb.at[t])
    load_w = local(4, w_hbm, wv)

    near = [partner, xdev, core]
    if nz > 1:
        near += [zdev(1), zdev(-1)]
    if ny > 1:
        near += [ydev(1), ydev(-1)]
    barrier = pltpu.get_barrier_semaphore()
    for dev in near:
        pl.semaphore_signal(barrier, inc=1, device_id=dev, device_id_type=MESH)
    pl.semaphore_wait(barrier, len(near))

    hops = {("a", 1): up, ("a", -1): dn, ("b", 1): dn, ("b", -1): up}

    def z_block(chain, step):
        return 2 * at_z(step) + (h if chain == "a" else o)

    def z_send(chain, way, hop, i):
        if hop < hops[chain, way]:
            block = kv.at[z_block(chain, -way * hop), i]
            send(("kv", chain, way, hop + 1, i), block, block, zdev(way))

    ghops = {("a", 1): yup, ("a", -1): ydn, ("b", 1): ydn, ("b", -1): yup}
    halves = [pl.ds(i * (T // 2), T // 2) for i in range(2)]

    def y_piece(chain, step):
        return 2 * at_y(step) + (xl if chain == "a" else 1 - xl)

    def y_send(chain, way, hop, i):
        if hop < ghops[chain, way]:
            piece = gb.at[y_piece(chain, -way * hop), halves[i]]
            src = g_hbm.at[0, halves[i]] if chain == "a" and hop == 0 else piece
            send(("g", chain, way, hop + 1, i), src, piece, ydev(way))

    def x_send(i):
        send(("gx", i), g_hbm.at[0, halves[i]], gb.at[t, halves[i]], xdev)

    x_send(0)
    for i in range(2):
        y_send("a", 1, 0, i)
        y_send("a", -1, 0, i)
    send("k", k_hbm.at[0, :, ocols], kv.at[c, 0], partner)
    send("v", v_hbm.at[0, :, ocols], kv.at[c, 1], partner)
    x_send(1)
    send("q", q_hbm.at[0, :, ocols], q2.at[hrows], partner)
    for i, load in ((0, load_k), (1, load_v)):
        load.wait()
        z_send("a", 1, 0, i)
        z_send("a", -1, 0, i)

    lane = lax.broadcasted_iota(jnp.int32, (1, Q2), 1)
    is_first = lane < T
    pos = jnp.where(is_first, lane, lane - T)
    b0 = 2 * z
    bvec = jnp.where(is_first, b0, b0 + 1)

    def both(ref, k):
        return jnp.where(is_first, ref[k, b0], ref[k, b0 + 1])

    row_global = any_of([pos == both(offs, g) for g in range(GB)])
    picks = [both(pat, r) for r in range(pat.shape[0])]
    for cc in range(nctx):
        seen = any_of([row_global, jnp.abs(bvec - cc) <= 1] + [pick == cc for pick in picks])
        qb[cc] = jnp.where(seen, 0.0, LOWEST)

    def key_bias(cc, carry):
        row = lax.broadcasted_iota(jnp.int32, (T, 128), 0)
        kb[cc] = jnp.where(any_of([row == offs[g, cc] for g in range(GB)]), 0.0, LOWEST)
        return carry

    lax.fori_loop(0, nctx, key_bias, 0)
    mx[...] = jnp.full_like(mx, LOWEST)
    gh[...] = jnp.zeros_like(gh)
    lr[...] = jnp.zeros_like(lr)
    ot[...] = jnp.zeros_like(ot)

    def score(cc):
        s = nt(kv[cc, 0], q2[...])
        bias = kb[cc]
        row_bias = qb[cc]
        for sl in lanes:
            part = s[:, sl] + jnp.maximum(bias, row_bias[:, sl])
            sb[cc, :, sl] = part
            mx[:, sl] = jnp.maximum(mx[:, sl], jnp.max(part.reshape(T // 8, 8, 128), axis=0))

    def project(tt):
        cols = pl.ds(pl.multiple_of(tt * DC, DC), DC)
        gh[...] += nt(gb[tt], wv[:, cols])

    group_of = {step: max(abs(step) - 1, 0) for step in range(-dn, up + 1)}
    n_group = max(group_of.values()) + 1
    TOTAL, DOT, FACTOR = n_group, n_group + 1, n_group + 2

    def weigh(j):
        stat[j] = jnp.max(mx[...], axis=0, keepdims=True)
        if j:
            scale = jnp.exp2((stat[j - 1] - stat[j]) * (SCALE * LOG2E))
            ot[...] = ot[...] * scale
            lr[...] = lr[...] * scale

        def one(cc):
            for sl in lanes:
                e = jnp.exp2((sb[cc, :, sl] - stat[j, :, sl]) * (SCALE * LOG2E))
                sb[cc, :, sl] = e
                lr[:, sl] += jnp.sum(e.reshape(T // 8, 8, 128), axis=0)
                pb[:, sl] = e.astype(BF16)
            ot[...] += tn(kv[cc, 1], pb[...])

        for step in [step for step, group in group_of.items() if group == j]:

            def pair(x, carry, step=step):
                one(2 * at_z(step) + x)
                return carry

            lax.fori_loop(0, 2, pair, 0)

    ready = {"q": False, "blocks": []}
    missing = {j: sum(4 for group in group_of.values() if group == j) for j in range(n_group)}

    def landed(step, count=1):
        missing[group_of[step]] -= count
        while missing and ready["q"] and missing[min(missing)] == 0:
            j = min(missing)
            del missing[j]
            weigh(j)

    def scores_of(cc):
        if ready["q"]:
            score(cc)
        else:
            ready["blocks"].append(cc)

    def on_own():
        load_g.wait()
        load_w.wait()
        project(t)
        scores_of(z_block("a", 0))
        landed(0, 2)

    def on_q():
        load_q.wait()
        arrive("q", q2.at[orows])
        ready["q"] = True
        for cc in ready["blocks"]:
            score(cc)
        landed(0, 0)

    def on_pair(i):
        pair = z_block("b", 0)
        arrive("kv"[i], kv.at[pair, i])
        z_send("b", 1, 0, i)
        z_send("b", -1, 0, i)
        if i == 0:
            scores_of(pair)
        landed(0)

    def on_gx(i):
        piece = y_piece("b", 0)
        arrive(("gx", i), gb.at[piece, halves[i]])
        y_send("b", 1, 0, i)
        y_send("b", -1, 0, i)
        if i:
            project(piece)

    def on_kv(chain, way, hop, i):
        step = -way * hop
        if step == -up:
            step = up
        block = z_block(chain, step)
        arrive(("kv", chain, way, hop, i), kv.at[block, i])
        z_send(chain, way, hop, i)
        if i == 0:
            scores_of(block)
        landed(step)

    def on_g(chain, way, hop, i):
        piece = y_piece(chain, -way * hop)
        arrive(("g", chain, way, hop, i), gb.at[piece, halves[i]])
        y_send(chain, way, hop, i)
        if i:
            project(piece)

    us = 2.0 / 88e3
    kv_us, g_us = T * HD * 2 * us, T * DC * us
    flows = {("gx", 0): ((), 0, "x", g_us, 1.8)}
    events = {("gx", 0): functools.partial(on_gx, 0)}
    for i in range(2):
        flows["kv"[i]] = ((), 0, "x", kv_us, 2.6)
        events["kv"[i]] = functools.partial(on_pair, i)
    flows["gx", 1] = ((), 0, "x", g_us, 1.8)
    events["gx", 1] = functools.partial(on_gx, 1)
    flows["q"] = ((), 0, "x", kv_us, 2.6)
    events["q"] = on_q
    for i in range(2):
        for (chain, way), count in hops.items():
            for hop in range(1, count + 1):
                name = ("kv", chain, way, hop, i)
                first = () if chain == "a" else ("kv"[i],)
                needs = (("kv", chain, way, hop - 1, i),) if hop > 1 else first
                flows[name] = (needs, 0.1, ("z", way), kv_us, 1.9)
                events[name] = functools.partial(on_kv, chain, way, hop, i)
        for (chain, way), count in ghops.items():
            for hop in range(1, count + 1):
                name = ("g", chain, way, hop, i)
                first = () if chain == "a" else (("gx", i),)
                needs = (("g", chain, way, hop - 1, i),) if hop > 1 else first
                flows[name] = (needs, 0.1, ("y", way), g_us, 1.8)
                events[name] = functools.partial(on_g, chain, way, hop, i)
    times = arrival_times(flows)

    def gather(names):
        for name in sorted(names, key=times.get):
            events[name]()

    last_g = max([times[name] for name in events if name[0] in ("g", "gx")])
    on_own()
    gather([name for name in events if times[name] <= last_g])
    ghb[0] = gh[:, :HD].astype(BF16)
    ghb[1] = gh[:, HD:].astype(BF16)
    send("do", ghb.at[o], do2.at[hrows], partner)
    do2[hrows, :] = ghb[h]
    gather([name for name in events if times[name] > last_g])

    inverse = 1.0 / jnp.sum(lr[...], axis=0, keepdims=True)
    low = (ot[...] * inverse).astype(BF16)
    ob[...] = low
    send("att", ob.at[:, orows], att.at[h], partner)
    att[h] = ob[:, hrows]
    for j in range(n_group):
        back = jnp.exp2((stat[j] - stat[n_group - 1]) * (SCALE * LOG2E))
        stat[FACTOR + j] = inverse * back
    arrive("do", do2.at[orows])
    do_t = jnp.transpose(do2[...].astype(F32))
    stat[DOT] = jnp.sum(do_t * low.astype(F32), axis=0, keepdims=True)
    dqt[...] = jnp.zeros_like(dqt)

    def gradients(step):
        zz = at_z(step)
        factor = stat.at[FACTOR + group_of[step]]

        def one(x, carry):
            cc = 2 * zz + x
            dp = nt(kv[cc, 1], do2[...])
            for sl in lanes:
                p = sb[cc, :, sl] * factor[:, sl]
                pb[:, sl] = p.astype(BF16)
                db[:, sl] = (p * (dp[:, sl] - stat[DOT, :, sl])).astype(BF16)
            own[zz, 0, x] = SCALE * nn(db[...], q2[...])
            own[zz, 1, x] = nn(pb[...], do2[...])
            dqt[...] += tn(kv[cc, 0], db[...])
            return carry

        lax.fori_loop(0, 2, one, 0)

    first_hop = {(0, 1): up, (0, -1): dn, (1, 1): dn, (1, -1): up}
    slots = {1: rp, -1: rm}

    def pass_on(i, way, hop):
        zz = at_z(way * hop)
        total = own[zz, i]
        if hop < first_hop[i, way]:
            slot = slots[way].at[i, hop]
            arrive(("kvg", i, way, hop + 1), slot)
            total = total + slot[...].astype(F32)
        snd[zz, i] = total.astype(BF16)
        send(("kvg", i, way, hop), snd.at[zz, i], slots[way].at[i, hop - 1], zdev(way))

    half = ntp // 2
    per_piece = DC // CW

    def weight_part(part, base, out):
        piece = base * half + part
        for head in range(2):
            rows = slice(head * HD, (head + 1) * HD)
            res = nn(att[head], gb[piece])
            for j in range(per_piece):
                out[part * per_piece + j, rows] = res[:, j * CW:(j + 1) * CW].astype(out.dtype)

    def weight_other():
        arrive("att", att.at[o])
        for part in range(half):
            weight_part(part, 1 - d, gws)
            block = pl.ds(part * per_piece, per_piece)
            send(("gw", part), gws.at[block], gwr.at[block], core)

    def weight_own():
        def one(part, carry):
            weight_part(part, d, gwo)
            return carry

        lax.fori_loop(0, half, one, 0)

    def weight_cross():
        for part in range(half):
            arrive(("gw", part), gwr.at[pl.ds(part * per_piece, per_piece)])
        for step in order:
            zz = at_z(step)
            gxs[zz] = (gwo[2 * zz + o] + gwr[2 * zz + o].astype(F32)).astype(BF16)
            send(("gwx", step), gxs.at[zz], gxr.at[zz], partner)

    order = [up] if nz > 1 else []
    for hop in range(dn, 0, -1):
        order += [hop, -hop]
    order += [0]
    gslots = {1: gp, -1: gm}
    tops = {1: pl.ds(0, F // 2), -1: pl.ds(F // 2, F // 2)}

    def weight_total(step):
        zz = at_z(step)
        arrive(("gwx", step), gxr.at[zz])
        gwo[2 * zz + h] = gwo[2 * zz + h] + gwr[2 * zz + h].astype(F32) + gxr[zz].astype(F32)

    def weight_add(zz, way, hop):
        rows = tops[way] if hop == up else pl.ds(0, F)
        slot = gslots[way].at[hop - 1, rows]
        arrive(("gwz", way, hop), slot)
        gwo[2 * zz + h, rows] = gwo[2 * zz + h, rows] + slot[...].astype(F32)

    def weight_far():
        weight_total(up)
        zz = at_z(up)
        gsn[zz] = gwo[2 * zz + h].astype(BF16)
        for way in (1, -1):
            send(("gwz", way, up), gsn.at[zz, tops[way]], gslots[way].at[up - 1, tops[way]], zdev(way))

    def weight_pass(way, hop):
        weight_total(way * hop)
        zz = at_z(way * hop)
        weight_add(zz, way, hop + 1)
        gsn[zz] = gwo[2 * zz + h].astype(BF16)
        send(("gwz", way, hop), gsn.at[zz], gslots[way].at[hop - 1], zdev(way))

    def gradient_pair(hop):
        gradients(hop)
        gradients(-hop)

    def finish(i):
        out = (dk_hbm, dv_hbm)[i]
        total = own[z, i]
        for way in (1, -1):
            if first_hop[i, way] > 0:
                arrive(("kvg", i, way, 1), slots[way].at[i, 0])
                total = total + slots[way][i, 0].astype(F32)
        fin[i] = total.astype(BF16)
        send(("fin", i), fin.at[i, o], out.at[0, :, hcols], partner)
        outs.append(local(i, fin.at[i, h], out.at[0, :, hcols]))

    outs = []

    def finish_q():
        dqb[...] = jnp.transpose(SCALE * dqt[...]).astype(BF16)
        send("dq", dqb.at[orows], dq_hbm.at[0, :, hcols], partner)
        outs.append(local(2, dqb.at[hrows], dq_hbm.at[0, :, hcols]))

    def finish_weight():
        weight_total(0)
        if nz > 1:
            weight_add(z, 1, 1)
            weight_add(z, -1, 1)
        gout[...] = gwo[2 * z + h].astype(BF16)
        outs.append(local(3, gout, gw_hbm))

    part = functools.partial
    if nz > 1:
        gradients(up)
        pass_on(0, 1, up)
        pass_on(1, -1, up)
    if dn:
        gradient_pair(dn)
        pass_on(1, 1, dn)
        pass_on(0, -1, dn)
    work = [part(gradient_pair, hop) for hop in range(dn - 1, 0, -1)]
    work += [part(gradients, 0), finish_q]
    if work:
        work.pop(0)()
    weight_other()
    weight_own()
    if dn:
        pass_on(0, 1, dn)
        pass_on(1, -1, dn)
    while work:
        work.pop(0)()
    weight_cross()
    tasks = []
    for hop in range(dn - 1, 0, -1):
        tasks += [part(pass_on, 1, 1, hop), part(pass_on, 0, -1, hop)]
        tasks += [part(pass_on, 0, 1, hop), part(pass_on, 1, -1, hop)]
    tasks += [part(finish, 1), part(finish, 0)] if dn else [part(finish, 0), part(finish, 1)]
    more = [weight_far] if nz > 1 else []
    for hop in range(dn, 0, -1):
        more += [part(weight_pass, 1, hop), part(weight_pass, -1, hop)]
    for i, task in enumerate(tasks):
        task()
        if i >= 3 and more and i % 2 == 1:
            for task in more[:1 if more[0] is weight_far else 2]:
                task()
                more.pop(0)
    for task in more:
        task()
    finish_weight()

    arrive("dq", dq_hbm.at[0, :, ocols])
    arrive(("fin", 0), dk_hbm.at[0, :, ocols])
    arrive(("fin", 1), dv_hbm.at[0, :, ocols])
    for cp in outs:
        cp.wait()
    for cp in sent:
        cp.wait_send()
    assert len(sem.index) <= N_SEM


def hand_on(*refs):
    n = (len(refs) - 1) // 3
    ins, outs, bufs, sems = refs[:n], refs[n:2 * n], refs[2 * n:3 * n], refs[3 * n]
    reads = [pltpu.make_async_copy(a, b, sems.at[i]) for i, (a, b) in enumerate(zip(ins, bufs))]
    writes = [pltpu.make_async_copy(a, b, sems.at[n + i]) for i, (a, b) in enumerate(zip(bufs, outs))]
    for cp in reads:
        cp.start()
    for read, write in zip(reads, writes):
        read.wait()
        write.start()
    for cp in writes:
        cp.wait()


def per_device(nz, ny, q, k, v, g, w, pattern, offsets):
    T = q.shape[1]
    Q2 = 2 * T
    nctx, ntp = 2 * nz, 2 * ny
    DC, F = g.shape[2], w.shape[0]
    CW = w.shape[1] // (2 * nctx)
    deep = max(nz // 2, 1)
    V = pltpu.VMEM
    hbm = pl.BlockSpec(memory_space=pl.ANY)
    smem = pl.BlockSpec(memory_space=pltpu.SMEM)
    scratch = [
        V((nctx, 2, T, HD), BF16),
        V((Q2, HD), BF16),
        V((Q2, HD), BF16),
        V((ntp, T, DC), BF16),
        V(w.shape, BF16),
        V((T, F), F32),
        V((2, T, HD), BF16),
        V((nctx, T, 128), F32),
        V((nctx, 1, Q2), F32),
        V((nctx, T, Q2), F32),
        V((8, Q2), F32),
        V((8, Q2), F32),
        V((2 * deep + 4, 1, Q2), F32),
        V((HD, Q2), F32),
        V((HD, Q2), BF16),
        V((2, HD, T), BF16),
        V((T, Q2), BF16),
        V((T, Q2), BF16),
        V((nz, 2, 2, T, HD), F32),
        V((nz, 2, 2, T, HD), BF16),
        V((2, deep, 2, T, HD), BF16),
        V((2, deep, 2, T, HD), BF16),
        V((HD, Q2), F32),
        V((Q2, HD), BF16),
        V((2, 2, T, HD), BF16),
        V((nctx, F, CW), BF16),
        V((nctx, F, CW), BF16),
        V((nctx, F, CW), F32),
        V((nz, F, CW), BF16),
        V((nz, F, CW), BF16),
        V((nz, F, CW), BF16),
        V((deep, F, CW), BF16),
        V((deep, F, CW), BF16),
        V((F, CW), BF16),
        pltpu.SemaphoreType.DMA((N_SEM,)),
        pltpu.SemaphoreType.DMA((N_SEM,)),
        pltpu.SemaphoreType.DMA((5,)),
    ]
    like = jax.ShapeDtypeStruct(q.shape, BF16)
    shapes = (like, like, like, jax.ShapeDtypeStruct((F, CW), BF16))
    results = pl.pallas_call(
        functools.partial(kernel, nz, ny),
        out_shape=shapes,
        in_specs=[smem, smem, hbm, hbm, hbm, hbm, hbm],
        out_specs=(hbm, hbm, hbm, hbm),
        scratch_shapes=scratch,
        compiler_params=pltpu.CompilerParams(
            collective_id=0, has_side_effects=True, vmem_limit_bytes=60 * 1024 * 1024
        ),
        name="attention_backward",
    )(pattern.T, offsets.T, q, k, v, g, w)
    return tuple(
        pl.pallas_call(
            hand_on,
            out_shape=shapes,
            in_specs=[hbm] * 4,
            out_specs=(hbm,) * 4,
            scratch_shapes=[V(s.shape, BF16) for s in shapes] + [pltpu.SemaphoreType.DMA((8,))],
            name="hand_on",
        )(*results)
    )


def solution(mesh):
    nz, ny = mesh.shape["ctx"] // 2, mesh.shape["tp"] // 2
    spec = P("dp", "ctx", "tp")
    return jax.shard_map(
        functools.partial(per_device, nz, ny),
        mesh=mesh,
        in_specs=(spec, spec, spec, spec, P("tp", None), P(), P()),
        out_specs=(spec, spec, spec, P("tp", ("dp", "ctx"))),
        check_vma=False,
    )
```

time: 102 us -> 74.2 us (0.73)
  Pallas kernels: 92.6 us -> 72.8 us
  local copies, waits for them, and re-layouts: 8.88 us -> 0 us
    pallas_call x1 -> x2, Pallas kernels: 92.6 us -> 72.8 us  [the longest x1 71 us: per_device(): pl.pallas_call(functools.partial(kernel, nz, ny), out_shape=shapes, in_sp...]
    unnamed x6 -> x0, local copies, waits for them, and re-layouts: 8.88 us -> none
where the time goes in v1:
time: 74.2 us; the launch traced here: 73.4 us
  Pallas kernels  72.8 us (98%)
    pallas_call x1, Pallas kernels, per_device(): pl.pallas_call(functools.partial(kernel, nz, ny), out_shape=shapes, in_sp...  71 us
    pallas_call x1, Pallas kernels, per_device(): pl.pallas_call(hand_on, out_shape=shapes, in_specs=[hbm] * 4, out_specs=(...  1.77 us

profile of v1, /device:TPU:2, one launch (start us, length us, event | category | flops | bytes accessed | tf_op | source)
XLA Modules:
  0.0 73.4 jit_solution(8445281204407498277)
XLA Ops:
  0.6 71.0 %attention_backward.1 = (bf16[1,256,256]{2,1,0:T(8,128)(2,1)}, bf16[1,256,256]{2,1,0:T(8,128)(2,1)}, bf16[1,256,256]{2,1,0:T(8,128)(2,1)}, bf16[256,128]{1,0:T(8,128)(2,1)}) custom-call(s32[3,16]{1,0:T(4,128)} %bitcast.3, s32[8,16]{1,0:T(8,128)} %bitcast.2, bf16[1,256,256]{2,1,0:T(8,128)(2,1)} %q_hbm.1, bf16[1,256,256]{2,1,0:T(8,128)(2,1)} %k_hbm.1, ...), custom_call_target="tpu_custom_call" | custom-call | tf_op jit(solution)/shard_map/attention_backward/pallas_call | solution.py:657
  71.6 1.8 %hand_on.1 = (bf16[1,256,256]{2,1,0:T(8,128)(2,1)}, bf16[1,256,256]{2,1,0:T(8,128)(2,1)}, bf16[1,256,256]{2,1,0:T(8,128)(2,1)}, bf16[256,128]{1,0:T(8,128)(2,1)}) custom-call(bf16[1,256,256]{2,1,0:T(8,128)(2,1)} %get-tuple-element.8.refs_0_, bf16[1,256,256]{2,1,0:T(8,128)(2,1)} %get-tuple-element.9.refs_1_, bf16[1,256,256]{2,1,0:T(8,128)(2,1)} %get-tuple-element.10.refs_2_, ...), custom_call_target="tpu_custom_call" | custom-call | tf_op jit(solution)/shard_map/hand_on/pallas_call | solution.py:669

commit v2 on v1

--- a/solution.py
+++ b/solution.py
@@ -40,7 +40,7 @@
         return self.index.setdefault(name, len(self.index))
 
 
-N_SEM = 110
+N_SEM = 140
 
 
 def arrival_times(flows):
@@ -136,8 +136,8 @@
     def at_y(step):
         return lax.rem(y + (step + ny), ny)
 
-    def zdev(step):
-        return (d, at_z(step) * 2 + h, t)
+    def zdev(step, column=None):
+        return (d, at_z(step) * 2 + (h if column is None else column), t)
 
     def ydev(step):
         return (d, c, at_y(step) * 2 + xl)
@@ -190,24 +190,28 @@
         pl.semaphore_signal(barrier, inc=1, device_id=dev, device_id_type=MESH)
     pl.semaphore_wait(barrier, len(near))
 
+    halves = [pl.ds(i * (T // 2), T // 2) for i in range(2)]
+
     hops = {("a", 1): up, ("a", -1): dn, ("b", 1): dn, ("b", -1): up}
 
     def z_block(chain, step):
         return 2 * at_z(step) + (h if chain == "a" else o)
 
-    def z_send(chain, way, hop, i):
+    def z_send(chain, way, hop, i, j):
         if hop < hops[chain, way]:
-            block = kv.at[z_block(chain, -way * hop), i]
-            send(("kv", chain, way, hop + 1, i), block, block, zdev(way))
-
-    ghops = {("a", 1): yup, ("a", -1): ydn, ("b", 1): ydn, ("b", -1): yup}
-    halves = [pl.ds(i * (T // 2), T // 2) for i in range(2)]
+            block = kv.at[z_block(chain, -way * hop), i, halves[j]]
+            send(("kv", chain, way, hop + 1, i, j), block, block, zdev(way))
 
     def y_piece(chain, step):
         return 2 * at_y(step) + (xl if chain == "a" else 1 - xl)
 
+    def y_goes(chain, way, hop, i):
+        if hop < yup:
+            return True
+        return hop == yup and chain == "a" and i == (0 if way == 1 else 1)
+
     def y_send(chain, way, hop, i):
-        if hop < ghops[chain, way]:
+        if y_goes(chain, way, hop + 1, i):
             piece = gb.at[y_piece(chain, -way * hop), halves[i]]
             src = g_hbm.at[0, halves[i]] if chain == "a" and hop == 0 else piece
             send(("g", chain, way, hop + 1, i), src, piece, ydev(way))
@@ -215,18 +219,20 @@
     def x_send(i):
         send(("gx", i), g_hbm.at[0, halves[i]], gb.at[t, halves[i]], xdev)
 
-    x_send(0)
+    for i, src in ((0, k_hbm), (1, v_hbm)):
+        for j in range(2):
+            send(("kv"[i], j), src.at[0, halves[j], ocols], kv.at[c, i, halves[j]], partner)
     for i in range(2):
         y_send("a", 1, 0, i)
-        y_send("a", -1, 0, i)
-    send("k", k_hbm.at[0, :, ocols], kv.at[c, 0], partner)
-    send("v", v_hbm.at[0, :, ocols], kv.at[c, 1], partner)
+        y_send("a", -1, 0, 1 - i)
+    x_send(0)
     x_send(1)
     send("q", q_hbm.at[0, :, ocols], q2.at[hrows], partner)
     for i, load in ((0, load_k), (1, load_v)):
         load.wait()
-        z_send("a", 1, 0, i)
-        z_send("a", -1, 0, i)
+        for j in range(2):
+            z_send("a", 1, 0, i, j)
+            z_send("a", -1, 0, i, j)
 
     lane = lax.broadcasted_iota(jnp.int32, (1, Q2), 1)
     is_first = lane < T
@@ -295,7 +301,7 @@
             lax.fori_loop(0, 2, pair, 0)
 
     ready = {"q": False, "blocks": []}
-    missing = {j: sum(4 for group in group_of.values() if group == j) for j in range(n_group)}
+    missing = {j: sum(8 for group in group_of.values() if group == j) for j in range(n_group)}
 
     def landed(step, count=1):
         missing[group_of[step]] -= count
@@ -315,7 +321,7 @@
         load_w.wait()
         project(t)
         scores_of(z_block("a", 0))
-        landed(0, 2)
+        landed(0, 4)
 
     def on_q():
         load_q.wait()
@@ -325,12 +331,12 @@
             score(cc)
         landed(0, 0)
 
-    def on_pair(i):
+    def on_pair(i, j):
         pair = z_block("b", 0)
-        arrive("kv"[i], kv.at[pair, i])
-        z_send("b", 1, 0, i)
-        z_send("b", -1, 0, i)
-        if i == 0:
+        arrive(("kv"[i], j), kv.at[pair, i, halves[j]])
+        z_send("b", 1, 0, i, j)
+        z_send("b", -1, 0, i, j)
+        if i == 0 and j == 1:
             scores_of(pair)
         landed(0)
 
@@ -342,57 +348,78 @@
         if i:
             project(piece)
 
-    def on_kv(chain, way, hop, i):
+    def on_kv(chain, way, hop, i, j):
         step = -way * hop
         if step == -up:
             step = up
         block = z_block(chain, step)
-        arrive(("kv", chain, way, hop, i), kv.at[block, i])
-        z_send(chain, way, hop, i)
-        if i == 0:
+        arrive(("kv", chain, way, hop, i, j), kv.at[block, i, halves[j]])
+        z_send(chain, way, hop, i, j)
+        if i == 0 and j == 1:
             scores_of(block)
         landed(step)
 
+    pieces = {}
+
+    def piece_half(chain, step):
+        step = yup if step == -yup else step
+        pieces[chain, step] = pieces.get((chain, step), 0) + 1
+        if pieces[chain, step] == 2:
+            project(y_piece(chain, step))
+
     def on_g(chain, way, hop, i):
-        piece = y_piece(chain, -way * hop)
-        arrive(("g", chain, way, hop, i), gb.at[piece, halves[i]])
+        step = yup if hop == yup else -way * hop
+        here = gb.at[y_piece(chain, step), halves[i]]
+        arrive(("g", chain, way, hop, i), here)
         y_send(chain, way, hop, i)
-        if i:
-            project(piece)
+        if hop == yup:
+            send(("gc", i), here, here, xdev)
+        piece_half(chain, step)
+
+    def on_gc(i):
+        arrive(("gc", i), gb.at[y_piece("b", yup), halves[i]])
+        piece_half("b", yup)
 
     us = 2.0 / 88e3
     kv_us, g_us = T * HD * 2 * us, T * DC * us
-    flows = {("gx", 0): ((), 0, "x", g_us, 1.8)}
-    events = {("gx", 0): functools.partial(on_gx, 0)}
+    part = functools.partial
+    flows, events = {}, {}
+
+    def flow(name, needs, delay, link, busy, wait, event):
+        flows[name] = (needs, delay, link, busy, wait)
+        events[name] = event
+
     for i in range(2):
-        flows["kv"[i]] = ((), 0, "x", kv_us, 2.6)
-        events["kv"[i]] = functools.partial(on_pair, i)
-    flows["gx", 1] = ((), 0, "x", g_us, 1.8)
-    events["gx", 1] = functools.partial(on_gx, 1)
-    flows["q"] = ((), 0, "x", kv_us, 2.6)
-    events["q"] = on_q
+        for j in range(2):
+            flow(("kv"[i], j), (), 0, "x", kv_us / 2, 2.6, part(on_pair, i, j))
+    for i in range(2):
+        flow(("gx", i), (), 0, "x", g_us, 1.8, part(on_gx, i))
+    flow("q", (), 0, "x", kv_us, 2.6, on_q)
     for i in range(2):
         for (chain, way), count in hops.items():
-            for hop in range(1, count + 1):
-                name = ("kv", chain, way, hop, i)
-                first = () if chain == "a" else ("kv"[i],)
-                needs = (("kv", chain, way, hop - 1, i),) if hop > 1 else first
-                flows[name] = (needs, 0.1, ("z", way), kv_us, 1.9)
-                events[name] = functools.partial(on_kv, chain, way, hop, i)
-        for (chain, way), count in ghops.items():
-            for hop in range(1, count + 1):
-                name = ("g", chain, way, hop, i)
-                first = () if chain == "a" else (("gx", i),)
-                needs = (("g", chain, way, hop - 1, i),) if hop > 1 else first
-                flows[name] = (needs, 0.1, ("y", way), g_us, 1.8)
-                events[name] = functools.partial(on_g, chain, way, hop, i)
+            for hop, j in [(hop, j) for hop in range(1, count + 1) for j in range(2)]:
+                first = () if chain == "a" else (("kv"[i], j),)
+                needs = (("kv", chain, way, hop - 1, i, j),) if hop > 1 else first
+                name = ("kv", chain, way, hop, i, j)
+                flow(name, needs, 0.1, ("z", way), kv_us / 2, 2.2, part(on_kv, chain, way, hop, i, j))
+        for chain in "ab":
+            for way in (1, -1):
+                for hop in range(1, yup + 1):
+                    if y_goes(chain, way, hop, i):
+                        first = () if chain == "a" else (("gx", i),)
+                        needs = (("g", chain, way, hop - 1, i),) if hop > 1 else first
+                        late = 0.2 if i == (0 if way == -1 else 1) else 0.1
+                        name = ("g", chain, way, hop, i)
+                        flow(name, needs, late, ("y", way), g_us, 1.8, part(on_g, chain, way, hop, i))
+                        if hop == yup:
+                            flow(("gc", i), (name,), 0.1, "x", g_us, 1.8, part(on_gc, i))
     times = arrival_times(flows)
 
     def gather(names):
         for name in sorted(names, key=times.get):
             events[name]()
 
-    last_g = max([times[name] for name in events if name[0] in ("g", "gx")])
+    last_g = max([times[name] for name in events if name[0] in ("g", "gx", "gc")])
     on_own()
     gather([name for name in events if times[name] <= last_g])
     ghb[0] = gh[:, :HD].astype(BF16)
@@ -530,7 +557,7 @@
     def finish_q():
         dqb[...] = jnp.transpose(SCALE * dqt[...]).astype(BF16)
         send("dq", dqb.at[orows], dq_hbm.at[0, :, hcols], partner)
-        outs.append(local(2, dqb.at[hrows], dq_hbm.at[0, :, hcols]))
+        outs.append(local(4, dqb.at[hrows], dq_hbm.at[0, :, hcols]))
 
     def finish_weight():
         weight_total(0)
@@ -538,9 +565,8 @@
             weight_add(z, 1, 1)
             weight_add(z, -1, 1)
         gout[...] = gwo[2 * z + h].astype(BF16)
-        outs.append(local(3, gout, gw_hbm))
-
-    part = functools.partial
+        outs.append(local(5, gout, gw_hbm))
+
     if nz > 1:
         gradients(up)
         pass_on(0, 1, up)
@@ -650,7 +676,7 @@
         V((F, CW), BF16),
         pltpu.SemaphoreType.DMA((N_SEM,)),
         pltpu.SemaphoreType.DMA((N_SEM,)),
-        pltpu.SemaphoreType.DMA((5,)),
+        pltpu.SemaphoreType.DMA((6,)),
     ]
     like = jax.ShapeDtypeStruct(q.shape, BF16)
     shapes = (like, like, like, jax.ShapeDtypeStruct((F, CW), BF16))

time: 74.2 us -> 71.9 us (0.969)
  Pallas kernels: 72.8 us -> 70.4 us
    pallas_call x1, Pallas kernels: 71 us -> 68.6 us  [per_device(): pl.pallas_call(functools.partial(kernel, nz, ny), out_shape=shapes, in_sp...]
where the time goes in v2:
time: 71.9 us; the launch traced here: 71.1 us
  Pallas kernels  70.4 us (98%)
    pallas_call x1, Pallas kernels, per_device(): pl.pallas_call(functools.partial(kernel, nz, ny), out_shape=shapes, in_sp...  68.6 us
    pallas_call x1, Pallas kernels, per_device(): pl.pallas_call(hand_on, out_shape=shapes, in_specs=[hbm] * 4, out_specs=(...  1.77 us

profile of v2, /device:TPU:2, one launch (start us, length us, event | category | flops | bytes accessed | tf_op | source)
XLA Modules:
  0.0 71.1 jit_solution(1984614795146349929)
XLA Ops:
  0.6 68.6 %attention_backward.1 = (bf16[1,256,256]{2,1,0:T(8,128)(2,1)}, bf16[1,256,256]{2,1,0:T(8,128)(2,1)}, bf16[1,256,256]{2,1,0:T(8,128)(2,1)}, bf16[256,128]{1,0:T(8,128)(2,1)}) custom-call(s32[3,16]{1,0:T(4,128)} %bitcast.3, s32[8,16]{1,0:T(8,128)} %bitcast.2, bf16[1,256,256]{2,1,0:T(8,128)(2,1)} %q_hbm.1, bf16[1,256,256]{2,1,0:T(8,128)(2,1)} %k_hbm.1, ...), custom_call_target="tpu_custom_call" | custom-call | tf_op jit(solution)/shard_map/attention_backward/pallas_call | solution.py:683
  69.3 1.8 %hand_on.1 = (bf16[1,256,256]{2,1,0:T(8,128)(2,1)}, bf16[1,256,256]{2,1,0:T(8,128)(2,1)}, bf16[1,256,256]{2,1,0:T(8,128)(2,1)}, bf16[256,128]{1,0:T(8,128)(2,1)}) custom-call(bf16[1,256,256]{2,1,0:T(8,128)(2,1)} %get-tuple-element.8.refs_0_, bf16[1,256,256]{2,1,0:T(8,128)(2,1)} %get-tuple-element.9.refs_1_, bf16[1,256,256]{2,1,0:T(8,128)(2,1)} %get-tuple-element.10.refs_2_, ...), custom_call_target="tpu_custom_call" | custom-call | tf_op jit(solution)/shard_map/hand_on/pallas_call | solution.py:695

commit v3 on v2

--- a/solution.py
+++ b/solution.py
@@ -40,7 +40,8 @@
         return self.index.setdefault(name, len(self.index))
 
 
-N_SEM = 140
+N_SEM = 160
+EARLY = 1
 
 
 def arrival_times(flows):
@@ -111,6 +112,7 @@
     ss,
     rs,
     ls,
+    here,
 ):
     T = q_hbm.shape[1]
     Q2 = 2 * T
@@ -180,7 +182,7 @@
     load_g = local(3, g_hbm.at[0], gb.at[t])
     load_w = local(4, w_hbm, wv)
 
-    near = [partner, xdev, core]
+    near = [partner, xdev]
     if nz > 1:
         near += [zdev(1), zdev(-1)]
     if ny > 1:
@@ -188,7 +190,17 @@
     barrier = pltpu.get_barrier_semaphore()
     for dev in near:
         pl.semaphore_signal(barrier, inc=1, device_id=dev, device_id_type=MESH)
-    pl.semaphore_wait(barrier, len(near))
+
+    @pl.when(d == 0)
+    def _():
+        pl.semaphore_signal(barrier, inc=1, device_id=core, device_id_type=MESH)
+
+    pl.semaphore_wait(barrier, len(near) + d)
+
+    @pl.when(d == 1)
+    def _():
+        pl.semaphore_signal(here, inc=1, device_id=core, device_id_type=MESH)
+
 
     halves = [pl.ds(i * (T // 2), T // 2) for i in range(2)]
 
@@ -464,46 +476,57 @@
 
     def pass_on(i, way, hop):
         zz = at_z(way * hop)
-        total = own[zz, i]
-        if hop < first_hop[i, way]:
-            slot = slots[way].at[i, hop]
-            arrive(("kvg", i, way, hop + 1), slot)
-            total = total + slot[...].astype(F32)
-        snd[zz, i] = total.astype(BF16)
-        send(("kvg", i, way, hop), snd.at[zz, i], slots[way].at[i, hop - 1], zdev(way))
+        for x in (o, h):
+            total = own[zz, i, x]
+            if hop < first_hop[i, way]:
+                slot = slots[way].at[i, hop, x]
+                arrive(("kvg", i, way, hop + 1, x is o), slot)
+                total = total + slot[...].astype(F32)
+            snd[zz, i, x] = total.astype(BF16)
+            send(("kvg", i, way, hop, x is o), snd.at[zz, i, x], slots[way].at[i, hop - 1, x], zdev(way))
 
     half = ntp // 2
     per_piece = DC // CW
 
-    def weight_part(part, base, out):
+    def weight_part(head, part, base, out):
         piece = base * half + part
-        for head in range(2):
-            rows = slice(head * HD, (head + 1) * HD)
-            res = nn(att[head], gb[piece])
-            for j in range(per_piece):
-                out[part * per_piece + j, rows] = res[:, j * CW:(j + 1) * CW].astype(out.dtype)
-
-    def weight_other():
-        arrive("att", att.at[o])
+        rows = pl.ds(pl.multiple_of(head * HD, HD), HD)
+        res = nn(att[head], gb[piece])
+        for j in range(per_piece):
+            out[part * per_piece + j, rows] = res[:, j * CW:(j + 1) * CW].astype(out.dtype)
+
+    def weight_other(phase):
+        head = o if phase else h
+        rows = pl.ds(pl.multiple_of(head * HD, HD), HD)
+        if phase:
+            arrive("att", att.at[o])
+        else:
+
+            @pl.when(d == 0)
+            def _():
+                pl.semaphore_wait(here, 1)
+
         for part in range(half):
-            weight_part(part, 1 - d, gws)
+            weight_part(head, part, 1 - d, gws)
             block = pl.ds(part * per_piece, per_piece)
-            send(("gw", part), gws.at[block], gwr.at[block], core)
-
-    def weight_own():
+            send(("gw", phase, part), gws.at[block, rows], gwr.at[block, rows], core)
+
+    def weight_own(phase):
         def one(part, carry):
-            weight_part(part, d, gwo)
+            weight_part(o if phase else h, part, d, gwo)
             return carry
 
         lax.fori_loop(0, half, one, 0)
 
-    def weight_cross():
+    def weight_cross(phase):
+        head = o if phase else h
+        rows = pl.ds(pl.multiple_of(head * HD, HD), HD)
         for part in range(half):
-            arrive(("gw", part), gwr.at[pl.ds(part * per_piece, per_piece)])
+            arrive(("gw", phase, part), gwr.at[pl.ds(part * per_piece, per_piece), rows])
         for step in order:
             zz = at_z(step)
-            gxs[zz] = (gwo[2 * zz + o] + gwr[2 * zz + o].astype(F32)).astype(BF16)
-            send(("gwx", step), gxs.at[zz], gxr.at[zz], partner)
+            gxs[zz, rows] = (gwo[2 * zz + o, rows] + gwr[2 * zz + o, rows].astype(F32)).astype(BF16)
+            send(("gwx", phase, step), gxs.at[zz, rows], gxr.at[zz, rows], partner)
 
     order = [up] if nz > 1 else []
     for hop in range(dn, 0, -1):
@@ -514,7 +537,10 @@
 
     def weight_total(step):
         zz = at_z(step)
-        arrive(("gwx", step), gxr.at[zz])
+        for phase in range(2):
+            head = h if phase else o
+            rows = pl.ds(pl.multiple_of(head * HD, HD), HD)
+            arrive(("gwx", phase, step), gxr.at[zz, rows])
         gwo[2 * zz + h] = gwo[2 * zz + h] + gwr[2 * zz + h].astype(F32) + gxr[zz].astype(F32)
 
     def weight_add(zz, way, hop):
@@ -541,16 +567,18 @@
         gradients(hop)
         gradients(-hop)
 
-    def finish(i):
+    def finish(i, x):
         out = (dk_hbm, dv_hbm)[i]
-        total = own[z, i]
+        total = own[z, i, x]
         for way in (1, -1):
             if first_hop[i, way] > 0:
-                arrive(("kvg", i, way, 1), slots[way].at[i, 0])
-                total = total + slots[way][i, 0].astype(F32)
-        fin[i] = total.astype(BF16)
-        send(("fin", i), fin.at[i, o], out.at[0, :, hcols], partner)
-        outs.append(local(i, fin.at[i, h], out.at[0, :, hcols]))
+                arrive(("kvg", i, way, 1, x is o), slots[way].at[i, 0, x])
+                total = total + slots[way][i, 0, x].astype(F32)
+        fin[i, x] = total.astype(BF16)
+        if x is o:
+            send(("fin", i), fin.at[i, o], out.at[0, :, hcols], partner)
+        else:
+            outs.append(local(i, fin.at[i, h], out.at[0, :, hcols]))
 
     outs = []
 
@@ -571,37 +599,48 @@
         gradients(up)
         pass_on(0, 1, up)
         pass_on(1, -1, up)
+    weight_other(0)
     if dn:
         gradient_pair(dn)
         pass_on(1, 1, dn)
         pass_on(0, -1, dn)
+    weight_own(0)
     work = [part(gradient_pair, hop) for hop in range(dn - 1, 0, -1)]
     work += [part(gradients, 0), finish_q]
-    if work:
-        work.pop(0)()
-    weight_other()
-    weight_own()
+    weight_cross(0)
+    weight_other(1)
     if dn:
         pass_on(0, 1, dn)
         pass_on(1, -1, dn)
-    while work:
-        work.pop(0)()
-    weight_cross()
+    work.pop(0)()
+    weight_own(1)
+    weight_cross(1)
     tasks = []
     for hop in range(dn - 1, 0, -1):
         tasks += [part(pass_on, 1, 1, hop), part(pass_on, 0, -1, hop)]
         tasks += [part(pass_on, 0, 1, hop), part(pass_on, 1, -1, hop)]
-    tasks += [part(finish, 1), part(finish, 0)] if dn else [part(finish, 0), part(finish, 1)]
+    ends = (1, 0) if dn else (0, 1)
     more = [weight_far] if nz > 1 else []
     for hop in range(dn, 0, -1):
         more += [part(weight_pass, 1, hop), part(weight_pass, -1, hop)]
     for i, task in enumerate(tasks):
         task()
-        if i >= 3 and more and i % 2 == 1:
+        if i == 1:
+            while work:
+                work.pop(0)()
+        if i % 2 == 1 and i >= EARLY and more:
             for task in more[:1 if more[0] is weight_far else 2]:
                 task()
                 more.pop(0)
-    for task in more:
+    while work:
+        work.pop(0)()
+    for i in ends:
+        finish(i, o)
+    for task in more[:-2]:
+        task()
+    for i in ends:
+        finish(i, h)
+    for task in more[-2:]:
         task()
     finish_weight()
 
@@ -677,6 +716,7 @@
         pltpu.SemaphoreType.DMA((N_SEM,)),
         pltpu.SemaphoreType.DMA((N_SEM,)),
         pltpu.SemaphoreType.DMA((6,)),
+        pltpu.SemaphoreType.REGULAR,
     ]
     like = jax.ShapeDtypeStruct(q.shape, BF16)
     shapes = (like, like, like, jax.ShapeDtypeStruct((F, CW), BF16))

time: 71.9 us -> 70.9 us (0.986)
  no operation moved by 1% of the time
where the time goes in v3:
time: 70.9 us; the launch traced here: 70.7 us
  Pallas kernels  70 us (99%)
    pallas_call x1, Pallas kernels, per_device(): pl.pallas_call(functools.partial(kernel, nz, ny), out_shape=shapes, in_sp...  68.2 us
    pallas_call x1, Pallas kernels, per_device(): pl.pallas_call(hand_on, out_shape=shapes, in_specs=[hbm] * 4, out_specs=(...  1.77 us

profile of v3, /device:TPU:2, one launch (start us, length us, event | category | flops | bytes accessed | tf_op | source)
XLA Modules:
  0.0 70.7 jit_solution(1300283977689726298)
XLA Ops:
  0.6 68.2 %attention_backward.1 = (bf16[1,256,256]{2,1,0:T(8,128)(2,1)}, bf16[1,256,256]{2,1,0:T(8,128)(2,1)}, bf16[1,256,256]{2,1,0:T(8,128)(2,1)}, bf16[256,128]{1,0:T(8,128)(2,1)}) custom-call(s32[3,16]{1,0:T(4,128)} %bitcast.3, s32[8,16]{1,0:T(8,128)} %bitcast.2, bf16[1,256,256]{2,1,0:T(8,128)(2,1)} %q_hbm.1, bf16[1,256,256]{2,1,0:T(8,128)(2,1)} %k_hbm.1, ...), custom_call_target="tpu_custom_call" | custom-call | tf_op jit(solution)/shard_map/attention_backward/pallas_call | solution.py:723
  68.9 1.8 %hand_on.1 = (bf16[1,256,256]{2,1,0:T(8,128)(2,1)}, bf16[1,256,256]{2,1,0:T(8,128)(2,1)}, bf16[1,256,256]{2,1,0:T(8,128)(2,1)}, bf16[256,128]{1,0:T(8,128)(2,1)}) custom-call(bf16[1,256,256]{2,1,0:T(8,128)(2,1)} %get-tuple-element.8.refs_0_, bf16[1,256,256]{2,1,0:T(8,128)(2,1)} %get-tuple-element.9.refs_1_, bf16[1,256,256]{2,1,0:T(8,128)(2,1)} %get-tuple-element.10.refs_2_, ...), custom_call_target="tpu_custom_call" | custom-call | tf_op jit(solution)/shard_map/hand_on/pallas_call | solution.py:735

commit v4 on v3

--- a/solution.py
+++ b/solution.py
@@ -296,21 +296,18 @@
             ot[...] = ot[...] * scale
             lr[...] = lr[...] * scale
 
-        def one(cc):
+        def one(cc, x):
             for sl in lanes:
                 e = jnp.exp2((sb[cc, :, sl] - stat[j, :, sl]) * (SCALE * LOG2E))
                 sb[cc, :, sl] = e
                 lr[:, sl] += jnp.sum(e.reshape(T // 8, 8, 128), axis=0)
-                pb[:, sl] = e.astype(BF16)
-            ot[...] += tn(kv[cc, 1], pb[...])
+                pb[x, :, sl] = e.astype(BF16)
+            ot[...] += tn(kv[cc, 1], pb[x])
 
         for step in [step for step, group in group_of.items() if group == j]:
 
-            def pair(x, carry, step=step):
-                one(2 * at_z(step) + x)
-                return carry
-
-            lax.fori_loop(0, 2, pair, 0)
+            one(2 * at_z(step), 0)
+            one(2 * at_z(step) + 1, 1)
 
     ready = {"q": False, "blocks": []}
     missing = {j: sum(8 for group in group_of.values() if group == j) for j in range(n_group)}
@@ -457,19 +454,19 @@
         zz = at_z(step)
         factor = stat.at[FACTOR + group_of[step]]
 
-        def one(x, carry):
+        def one(x):
             cc = 2 * zz + x
             dp = nt(kv[cc, 1], do2[...])
             for sl in lanes:
                 p = sb[cc, :, sl] * factor[:, sl]
-                pb[:, sl] = p.astype(BF16)
-                db[:, sl] = (p * (dp[:, sl] - stat[DOT, :, sl])).astype(BF16)
-            own[zz, 0, x] = SCALE * nn(db[...], q2[...])
-            own[zz, 1, x] = nn(pb[...], do2[...])
-            dqt[...] += tn(kv[cc, 0], db[...])
-            return carry
-
-        lax.fori_loop(0, 2, one, 0)
+                pb[x, :, sl] = p.astype(BF16)
+                db[x, :, sl] = (p * (dp[:, sl] - stat[DOT, :, sl])).astype(BF16)
+            own[zz, 0, x] = SCALE * nn(db[x], q2[...])
+            own[zz, 1, x] = nn(pb[x], do2[...])
+            dqt[...] += tn(kv[cc, 0], db[x])
+
+        one(0)
+        one(1)
 
     first_hop = {(0, 1): up, (0, -1): dn, (1, 1): dn, (1, -1): up}
     slots = {1: rp, -1: rm}
@@ -512,11 +509,8 @@
             send(("gw", phase, part), gws.at[block, rows], gwr.at[block, rows], core)
 
     def weight_own(phase):
-        def one(part, carry):
+        for part in range(half):
             weight_part(o if phase else h, part, d, gwo)
-            return carry
-
-        lax.fori_loop(0, half, one, 0)
 
     def weight_cross(phase):
         head = o if phase else h
@@ -695,8 +689,8 @@
         V((HD, Q2), F32),
         V((HD, Q2), BF16),
         V((2, HD, T), BF16),
-        V((T, Q2), BF16),
-        V((T, Q2), BF16),
+        V((2, T, Q2), BF16),
+        V((2, T, Q2), BF16),
         V((nz, 2, 2, T, HD), F32),
         V((nz, 2, 2, T, HD), BF16),
         V((2, deep, 2, T, HD), BF16),

time: 70.9 us -> 69.7 us (0.983)
  Pallas kernels: 70 us -> 68.7 us
    pallas_call x1, Pallas kernels: 68.2 us -> 67 us  [per_device(): pl.pallas_call(functools.partial(kernel, nz, ny), out_shape=shapes, in_sp...]
where the time goes in v4:
time: 69.7 us; the launch traced here: 69.5 us
  Pallas kernels  68.7 us (99%)
  between operations  0.8 us (1%)
    pallas_call x1, Pallas kernels, per_device(): pl.pallas_call(functools.partial(kernel, nz, ny), out_shape=shapes, in_sp...  67 us
    pallas_call x1, Pallas kernels, per_device(): pl.pallas_call(hand_on, out_shape=shapes, in_specs=[hbm] * 4, out_specs=(...  1.77 us

profile of v4, /device:TPU:2, one launch (start us, length us, event | category | flops | bytes accessed | tf_op | source)
XLA Modules:
  0.0 69.5 jit_solution(4129484966594133843)
XLA Ops:
  0.6 67.0 %attention_backward.1 = (bf16[1,256,256]{2,1,0:T(8,128)(2,1)}, bf16[1,256,256]{2,1,0:T(8,128)(2,1)}, bf16[1,256,256]{2,1,0:T(8,128)(2,1)}, bf16[256,128]{1,0:T(8,128)(2,1)}) custom-call(s32[3,16]{1,0:T(4,128)} %bitcast.3, s32[8,16]{1,0:T(8,128)} %bitcast.2, bf16[1,256,256]{2,1,0:T(8,128)(2,1)} %q_hbm.1, bf16[1,256,256]{2,1,0:T(8,128)(2,1)} %k_hbm.1, ...), custom_call_target="tpu_custom_call" | custom-call | tf_op jit(solution)/shard_map/attention_backward/pallas_call | solution.py:717
  67.6 1.8 %hand_on.1 = (bf16[1,256,256]{2,1,0:T(8,128)(2,1)}, bf16[1,256,256]{2,1,0:T(8,128)(2,1)}, bf16[1,256,256]{2,1,0:T(8,128)(2,1)}, bf16[256,128]{1,0:T(8,128)(2,1)}) custom-call(bf16[1,256,256]{2,1,0:T(8,128)(2,1)} %get-tuple-element.8.refs_0_, bf16[1,256,256]{2,1,0:T(8,128)(2,1)} %get-tuple-element.9.refs_1_, bf16[1,256,256]{2,1,0:T(8,128)(2,1)} %get-tuple-element.10.refs_2_, ...), custom_call_target="tpu_custom_call" | custom-call | tf_op jit(solution)/shard_map/hand_on/pallas_call | solution.py:729
